TPU v7x, 256 devices: a whole 4x4x8 slice. The times are simulated.
256 devices in a mesh: gx: 8 (over y, core), gy: 32 (over x, z).
Axes of the slice: x: 4, y: 4, z: 8, core: 2. Of those that a mesh axis runs over, the one named last changes fastest.
Arguments:
- control: float32 [1, 2, 6, 1536, 3072], P(None, None, None, 'gy', 'gx'), may hold values from -6 to 6
- sigma: float32 [2, 6, 1536, 3072], P(None, None, 'gy', 'gx'), may hold values from 0.5 to 5
- kappa: float32 [5, 1536, 3072], P(None, 'gy', 'gx'), may hold values from 0.05 to 5
- beta: float32 [6, 1536, 3072], P(None, 'gy', 'gx'), may hold values from -3 to 3
- sea_mask: int32 [1536, 3072], P('gy', 'gx'), may hold values 0 or 1
- x_inverse: float32 [3072, 3072], P('gx'), as said below
- y_inverse: float32 [1536, 1536], P('gx')
- ssh_coef: float32 [2, 6], replicated, may hold values from -1.5 to 1.5
- obs_owner: int32 [65536, 1], P(('gx', 'gy')), may hold values from 0 to 255; in each aligned block of 256 rows (0 to 255, 256 to 511, ...) at most 2 rows name the same one
- tile_index: int32 [65536], P(('gx', 'gy')), may hold values from 0 to 18046, as said below
- obs_frac: float32 [2, 65536], P(None, ('gx', 'gy')), may hold values from 0 to 1
- obs_count: int32 [256], P(('gx', 'gy')), may hold values from 128 to 256
Outputs:
- increments: float32 [1, 2, 6, 1536, 3072], P(None, None, None, 'gy', 'gx')
- sea_height: float32 [1, 1536, 3072], P(None, 'gy', 'gx')
- obs_equiv: float32 [2, 13, 65536], P(None, None, ('gx', 'gy'))
Inputs may be any that keep to these rules, and one draw needn't show every extreme that they name: `obs_owner`: among the slots of one device, at most 2 name the same owner. `tile_index`: row * 384 + column of a cell in the device's own tile, with row below 47 and column below 383. `x_inverse`: the zonal inverse is symmetric.
All inputs are finite; a program needn't handle non-finite values. No bound on the sum of `sea_mask` on one device may be relied on, other than what follows from the above.
Results may differ from a plain program's by a relative error of at most 0.00013.
Values sent between devices are 32-bit elements; how exact they have to be, the bound alone decides.
A program may use at most 128 MiB of HBM per device.

v0:
```python
import jax
import jax.numpy as jnp
from jax import lax
from jax.sharding import PartitionSpec as P

STEPS = 2
CAP = 2


def vertical(values, kappa):
    levels = values.shape[2]
    c_list = []
    d_list = []
    for level in range(levels):
        k_below = kappa[level - 1] if level > 0 else 0.0
        k_above = kappa[level] if level < levels - 1 else 0.0
        diag_term = 1.0 + k_below + k_above
        if level == 0:
            pivot = diag_term
            d_new = values[:, :, 0] / pivot
        else:
            pivot = diag_term + k_below * c_list[-1]
            d_new = (values[:, :, level] + k_below * d_list[-1]) / pivot
        c_list.append(-k_above / pivot)
        d_list.append(d_new)
    result = [d_list[-1]]
    for level in range(levels - 2, -1, -1):
        result.insert(0, d_list[level] - c_list[level] * result[0])
    return jnp.stack(result, axis=2)


def body(
    control,
    sigma,
    kappa,
    beta,
    sea_mask,
    x_inverse,
    y_inverse,
    ssh_coef,
    obs_owner,
    tile_index,
    obs_frac,
    obs_count,
):
    highest = lax.Precision.HIGHEST
    vec_count, kinds, levels, lat_rows, lon_cols = control.shape
    field_count = vec_count * kinds * levels
    sea_open = sea_mask.astype(jnp.float32)
    grid_field = control.reshape(field_count, lat_rows, lon_cols)
    whole_y = lax.all_gather(y_inverse, "gx", axis=0, tiled=True)
    for diffusion_step in range(STEPS):
        grid_field = sea_open * jnp.einsum(
            "fyb,ab->fya",
            lax.all_gather(grid_field, "gx", axis=2, tiled=True),
            x_inverse,
            precision=highest,
        )
        turned = jnp.swapaxes(grid_field, 1, 2)
        merid_lines = lax.all_to_all(turned, "gy", split_axis=1, concat_axis=2, tiled=True)
        solved = jnp.einsum("fxb,ab->fxa", merid_lines, whole_y, precision=highest)
        returned = lax.all_to_all(solved, "gy", split_axis=2, concat_axis=1, tiled=True)
        grid_field = sea_open * jnp.swapaxes(returned, 1, 2)
        grid_field = vertical(
            grid_field.reshape(vec_count, kinds, levels, lat_rows, lon_cols), kappa
        ).reshape(field_count, lat_rows, lon_cols)
    grid_field = grid_field.reshape(vec_count, kinds, levels, lat_rows, lon_cols)
    temper = sigma[0] * grid_field[:, 0]
    saline = sigma[1] * grid_field[:, 1] + beta * temper
    height = jnp.sum(
        ssh_coef[0][None, :, None, None] * temper + ssh_coef[1][None, :, None, None] * saline,
        axis=1,
    )
    increments = jnp.stack([temper, saline], axis=1)
    profile = jnp.concatenate([temper, saline, height[:, None]], axis=1)
    slot_total = tile_index.shape[0]
    row_index = tile_index // lon_cols
    col_index = tile_index % lon_cols
    frac_x = obs_frac[0]
    frac_y = obs_frac[1]
    corner_a = profile[:, :, row_index, col_index]
    corner_b = profile[:, :, row_index, col_index + 1]
    corner_c = profile[:, :, row_index + 1, col_index]
    corner_d = profile[:, :, row_index + 1, col_index + 1]
    interp = (1.0 - frac_y) * ((1.0 - frac_x) * corner_a + frac_x * corner_b) + frac_y * (
        (1.0 - frac_x) * corner_c + frac_x * corner_d
    )
    live_slot = (jnp.arange(slot_total, dtype=jnp.int32) < obs_count[0]).astype(jnp.float32)
    record_len = interp.shape[0] * interp.shape[1]
    interp = (interp * live_slot).reshape(record_len, slot_total)
    gx_count = lax.axis_size("gx")
    gy_count = lax.axis_size("gy")
    device_total = gx_count * gy_count
    owners = obs_owner[:, 0]
    one_hot = (owners[:, None] == jnp.arange(device_total, dtype=jnp.int32)[None, :]).astype(
        jnp.int32
    )
    before = jnp.cumsum(one_hot, axis=0) - one_hot
    slot_rank = jnp.sum(before * one_hot, axis=1)
    outgoing = (
        jnp.zeros((CAP, record_len, device_total), jnp.float32)
        .at[slot_rank, :, owners]
        .set(interp.T)
    )
    outgoing = outgoing.reshape(CAP, record_len, gx_count, gy_count)
    arrived = lax.all_to_all(
        lax.all_to_all(outgoing, "gx", split_axis=2, concat_axis=2, tiled=True),
        "gy",
        split_axis=3,
        concat_axis=3,
        tiled=True,
    )
    obs_equiv = arrived.reshape(CAP, record_len, device_total)
    return (increments, height, obs_equiv)


def solution(mesh):
    return jax.shard_map(
        body,
        mesh=mesh,
        in_specs=(
            P(None, None, None, "gy", "gx"),
            P(None, None, "gy", "gx"),
            P(None, "gy", "gx"),
            P(None, "gy", "gx"),
            P("gy", "gx"),
            P("gx", None),
            P("gx", None),
            P(),
            P(("gx", "gy"), None),
            P(("gx", "gy")),
            P(None, ("gx", "gy")),
            P(("gx", "gy")),
        ),
        out_specs=(
            P(None, None, None, "gy", "gx"),
            P(None, "gy", "gx"),
            P(None, None, ("gx", "gy")),
        ),
        check_vma=False,
    )
```

profile of v0, /device:TPU:1, one launch (start us, length us, event | category | flops | bytes accessed | tf_op | source)
XLA Modules:
  0.0 489.2 jit_solution(15231277766906948029)
XLA Ops:
  9.6 51.3 %all-gather.4.cloned.1.call-done = f32[12,48,3072]{2,1,0:T(8,128)} async-done(((f32[12,48,384]{2,1,0:T(8,128)}), f32[12,48,3072]{2,1,0:T(8,128)}) %all-gather.4.cloned.1.call-update) | async-done | bytes 7077904 | tf_op jit(solution)/shard_map/all_gather | solution.py:55
  60.9 15.1 %fusion.11 = f32[12,384,48]{1,2,0:T(8,128)} fusion(f32[12,48,3072]{2,1,0:T(8,128)} %all-gather.4.cloned.1.call-done, f32[384,3072]{1,0:T(8,128)} %param.17, f32[384,48]{0,1:T(8,128)S(1)} %get-tuple-element.41), kind=kOutput, calls=%fused_computation.16 | convolution fusion | flops 8153948160 | bytes 12754944 | tf_op jit(solution)/shard_map/fyb,ab->fya/dot_general | solution.py:53
  81.7 42.5 %all_to_all.82 = f32[32,1,6912]{2,1,0:T(1,128)S(1)} all-to-all(f32[32,1,6912]{2,1,0:T(1,128)} %reshape.729), channel_id=1, replica_groups=mesh['gx'=8,'gy'=32] {'gy'}, dimensions={0} | all-to-all | bytes 1769472 | tf_op jit(solution)/shard_map/all_to_all | solution.py:60
  137.4 12.0 %fusion.2 = f32[12,12,1536]{2,1,0:T(8,128)S(1)} fusion(f32[12,12,1536]{2,1,0:T(8,128)S(1)} %all_to_all.61, f32[1536,1536]{1,0:T(8,128)} %all-gather.6.cloned.1.call-done), kind=kOutput, calls=%fused_computation.7 | convolution fusion | flops 4076863488 | bytes 11206656 | tf_op jit(solution)/shard_map/fxb,ab->fxa/dot_general | solution.py:61
  149.4 8.6 %copy.95 = f32[12,12,1536]{1,0,2:T(8,128)} copy(f32[12,12,1536]{2,1,0:T(8,128)S(1)} %fusion.2) | data formatting | bytes 1769472 | tf_op jit(solution)/shard_map/fxb,ab->fxa/dot_general | solution.py:61
  158.0 10.0 %reshape.731 = f32[32,1,6912]{2,1,0:T(1,128)} reshape(f32[1536,12,12]{2,1,0:T(8,128)} %bitcast.172) | data formatting | bytes 1769472
  168.0 8.0 %all-to-all-start.1 = ((f32[32,1,6912]{2,1,0:T(1,128)}), f32[32,1,6912]{2,1,0:T(1,128)S(1)}, u32[]{:S(2)}, u32[]{:S(2)}) async-start(f32[32,1,6912]{2,1,0:T(1,128)} %reshape.731), calls=%async_computation.1 | async-start | bytes 1769472 | tf_op jit(solution)/shard_map/all_to_all | solution.py:62
  180.4 17.1 %all-to-all-done.1 = f32[32,1,6912]{2,1,0:T(1,128)S(1)} async-done(((f32[32,1,6912]{2,1,0:T(1,128)}), f32[32,1,6912]{2,1,0:T(1,128)S(1)}, u32[]{:S(2)}, u32[]{:S(2)}) %all-to-all-start.1) | async-done | bytes 884768 | tf_op jit(solution)/shard_map/all_to_all | solution.py:62
  200.2 8.0 %reshape.732 = f32[1536,12,12]{2,1,0:T(8,128)} reshape(f32[32,6912]{1,0:T(8,128)S(1)} %reduce.2) | data formatting | bytes 1769472
  208.2 9.7 %copy.96 = f32[12,12,32,48]{3,1,2,0:T(8,128)S(1)} copy(f32[12,12,32,48]{1,0,3,2:T(8,128)} %bitcast.174) | data formatting | bytes 1769472 | tf_op jit(solution)/shard_map/all_to_all | solution.py:62
  225.6 46.7 %all-gather.8.cloned.1.call-done = f32[12,48,3072]{2,1,0:T(8,128)} async-done(((f32[12,48,384]{2,1,0:T(8,128)}), f32[12,48,3072]{2,1,0:T(8,128)}) %all-gather.8.cloned.1.call-update) | async-done | bytes 7077904 | tf_op jit(solution)/shard_map/all_gather | solution.py:55
  272.4 15.1 %fusion.17 = f32[12,384,48]{1,2,0:T(8,128)} fusion(f32[12,48,3072]{2,1,0:T(8,128)} %all-gather.8.cloned.1.call-done, f32[384,3072]{1,0:T(8,128)} %param.17, f32[384,48]{0,1:T(8,128)S(1)} %copy-done.8), kind=kOutput, calls=%fused_computation.18 | convolution fusion | flops 8153948160 | bytes 12754944 | tf_op jit(solution)/shard_map/fyb,ab->fya/dot_general | solution.py:53
  293.1 9.7 %all-to-all-start.2 = ((f32[32,1,6912]{2,1,0:T(1,128)}), f32[32,1,6912]{2,1,0:T(1,128)S(1)}, u32[]{:S(2)}, u32[]{:S(2)}) async-start(f32[32,1,6912]{2,1,0:T(1,128)} %reshape.733), calls=%async_computation.2 | async-start | bytes 1769472 | tf_op jit(solution)/shard_map/all_to_all | solution.py:60
  303.9 20.3 %all-to-all-done.2 = f32[32,1,6912]{2,1,0:T(1,128)S(1)} async-done(((f32[32,1,6912]{2,1,0:T(1,128)}), f32[32,1,6912]{2,1,0:T(1,128)S(1)}, u32[]{:S(2)}, u32[]{:S(2)}) %all-to-all-start.2) | async-done | bytes 884768 | tf_op jit(solution)/shard_map/all_to_all | solution.py:60
  336.8 12.0 %fusion = f32[12,12,1536]{2,1,0:T(8,128)S(1)} fusion(f32[12,12,1536]{2,1,0:T(8,128)S(1)} %all_to_all.69, f32[1536,1536]{1,0:T(8,128)} %all-gather.6.cloned.1.call-done), kind=kOutput, calls=%fused_computation.5 | convolution fusion | flops 4076863488 | bytes 11206656 | tf_op jit(solution)/shard_map/fxb,ab->fxa/dot_general | solution.py:61
  348.8 8.8 %copy.101 = f32[12,12,1536]{1,0,2:T(8,128)} copy(f32[12,12,1536]{2,1,0:T(8,128)S(1)} %fusion) | data formatting | bytes 1769472 | tf_op jit(solution)/shard_map/fxb,ab->fxa/dot_general | solution.py:61
  357.7 10.0 %reshape.735 = f32[32,1,6912]{2,1,0:T(1,128)} reshape(f32[1536,12,12]{2,1,0:T(8,128)} %bitcast.173) | data formatting | bytes 1769472
  367.7 8.4 %all-to-all-start.3 = ((f32[32,1,6912]{2,1,0:T(1,128)}), f32[32,1,6912]{2,1,0:T(1,128)S(1)}, u32[]{:S(2)}, u32[]{:S(2)}) async-start(f32[32,1,6912]{2,1,0:T(1,128)} %reshape.735), calls=%async_computation.3 | async-start | bytes 1769472 | tf_op jit(solution)/shard_map/all_to_all | solution.py:62
  376.5 21.0 %all-to-all-done.3 = f32[32,1,6912]{2,1,0:T(1,128)S(1)} async-done(((f32[32,1,6912]{2,1,0:T(1,128)}), f32[32,1,6912]{2,1,0:T(1,128)S(1)}, u32[]{:S(2)}, u32[]{:S(2)}) %all-to-all-start.3) | async-done | bytes 884768 | tf_op jit(solution)/shard_map/all_to_all | solution.py:62
  400.3 7.6 %reshape.736 = f32[1536,12,12]{2,1,0:T(8,128)} reshape(f32[32,6912]{1,0:T(8,128)S(1)} %reduce.4) | data formatting | bytes 1769472
  407.9 9.7 %copy.102 = f32[12,12,32,48]{3,1,2,0:T(8,128)S(1)} copy(f32[12,12,32,48]{1,0,3,2:T(8,128)} %bitcast.175) | data formatting | bytes 1769472 | tf_op jit(solution)/shard_map/all_to_all | solution.py:62
  440.4 12.1 %scatter_fusion = f32[2,13,256]{1,2,0:T(8,128)S(1)} fusion(f32[2,13,256]{1,2,0:T(8,128)S(1)} %broadcast_in_dim.15, s32[256]{0:T(256)S(1)} %bitcast.176, f32[256,13]{1,0:T(8,128)S(1)} %copy.111), kind=kCustom, calls=%fused_computation.4 | custom fusion | bytes 41984 | tf_op jit(solution)/shard_map/scatter | solution.py:103
  452.8 12.6 %all_to_all.83 = f32[8,1,832]{2,1,0:T(1,128)S(1)} all-to-all(f32[8,1,832]{2,1,0:T(1,128)S(1)} %reshape.737), channel_id=1, replica_groups=mesh['gx'=8,'gy'=32] {'gx'}, dimensions={0} | all-to-all | bytes 53248 | tf_op jit(solution)/shard_map/all_to_all | solution.py:107
  472.7 7.8 %all-to-all-done.5 = f32[32,1,208]{2,1,0:T(1,128)S(1)} async-done(((f32[32,1,208]{2,1,0:T(1,128)}), f32[32,1,208]{2,1,0:T(1,128)S(1)}, u32[]{:S(2)}, u32[]{:S(2)}) %all-to-all-start.5) | async-done | bytes 26656 | tf_op jit(solution)/shard_map/all_to_all | solution.py:106
  (121 shorter events, 89.7 us)
Async XLA Ops:
  7.2 53.7 %all-gather.4.cloned.1.call-start = ((), (), s32[]{:S(2)}) async-start(), calls=%async_computation.6 | async-start | bytes 7962624 | tf_op jit(solution)/shard_map/all_gather | solution.py:55
  7.9 129.5 %all-gather.6.cloned.1.call-start = ((), (), s32[]{:S(2)}) async-start(), calls=%async_computation.7 | async-start | bytes 10616832 | tf_op jit(solution)/shard_map/all_gather | solution.py:51
  9.5 51.3 %copy-start.7 = (f32[384,48]{0,1:T(8,128)}, f32[384,48]{0,1:T(8,128)S(1)}, u32[]{:S(2)}) copy-start(f32[384,48]{0,1:T(8,128)S(1)} %get-tuple-element.41) | copy-start | bytes 221188
  158.0 18.9 %copy-start = (f32[5,48,384]{2,1,0:T(8,128)S(1)}, f32[5,48,384]{2,1,0:T(8,128)}, u32[]{:S(2)}) copy-start(f32[5,48,384]{2,1,0:T(8,128)} %param.14) | copy-start | bytes 1105924
  168.0 29.5 %all-to-all-start.1 = ((f32[32,1,6912]{2,1,0:T(1,128)}), f32[32,1,6912]{2,1,0:T(1,128)S(1)}, u32[]{:S(2)}, u32[]{:S(2)}) async-start(f32[32,1,6912]{2,1,0:T(1,128)} %reshape.731), calls=%async_computation.1 | async-start | bytes 1769472 | tf_op jit(solution)/shard_map/all_to_all | solution.py:62
  176.0 96.3 %all-gather.8.cloned.1.call-start = ((), (), s32[]{:S(2)}) async-start(), calls=%async_computation.8 | async-start | bytes 7962624 | tf_op jit(solution)/shard_map/all_gather | solution.py:55
  177.6 2.8 copy-start.3
  178.3 0.6 copy-start.2
  222.2 50.2 %copy-start.8 = (f32[384,48]{0,1:T(8,128)S(1)}, f32[384,48]{0,1:T(8,128)}, u32[]{:S(2)}) copy-start(f32[384,48]{0,1:T(8,128)} %copy-done.7) | copy-start | bytes 221188
  224.7 0.9 copy-start.1
  287.5 16.0 %copy-start.11 = (s32[256,1]{0,1:T(1,128)S(1)}, s32[256,1]{0,1:T(1,128)}, u32[]{:S(2)}) copy-start(s32[256,1]{0,1:T(1,128)} %param.20) | copy-start | bytes 3076
  293.1 31.1 %all-to-all-start.2 = ((f32[32,1,6912]{2,1,0:T(1,128)}), f32[32,1,6912]{2,1,0:T(1,128)S(1)}, u32[]{:S(2)}, u32[]{:S(2)}) async-start(f32[32,1,6912]{2,1,0:T(1,128)} %reshape.733), calls=%async_computation.2 | async-start | bytes 1769472 | tf_op jit(solution)/shard_map/all_to_all | solution.py:60
  303.8 20.4 %copy-start.4 = (s32[256,2,128]{0,1,2:T(2,128)}, s32[256,2,128]{0,1,2:T(2,128)S(1)}, u32[]{:S(2)}) copy-start(s32[256,2,128]{0,1,2:T(2,128)S(1)} %fusion.23) | copy-start | bytes 786436
  303.9 29.8 %copy-start.12 = (s32[256,3]{0,1:T(4,128)}, s32[256,3]{0,1:T(4,128)S(1)}, u32[]{:S(2)}) copy-start(s32[256,3]{0,1:T(4,128)S(1)} %reduce-window.9) | copy-start | bytes 9220
  357.7 18.4 %slice-start = ((s32[256,3]{0,1:T(4,128)}), s32[256,2]{0,1:T(2,128)S(1)}, s32[]{:S(2)}) async-start(s32[256,3]{0,1:T(4,128)} %copy-done.12), calls=%async_computation.9 | async-start | bytes 4096 | tf_op jit(solution)/shard_map/slice.1
  357.7 18.4 %copy-start.5 = (s32[256,2,128]{0,1,2:T(2,128)S(1)}, s32[256,2,128]{0,1,2:T(2,128)}, u32[]{:S(2)}) copy-start(s32[256,2,128]{0,1,2:T(2,128)} %copy-done.4) | copy-start | bytes 786436
  357.7 18.7 %copy-start.15 = (f32[2,6]{1,0:T(2,128)S(1)}, f32[2,6]{1,0:T(2,128)}, u32[]{:S(2)}) copy-start(f32[2,6]{1,0:T(2,128)} %param.19) | copy-start | bytes 148
  357.7 18.7 %copy-start.13 = (s32[256]{0:T(256)S(1)}, s32[256]{0:T(256)}, u32[]{:S(2)}) copy-start(s32[256]{0:T(256)} %param.21) | copy-start | bytes 3076
  357.7 18.7 %copy-start.14 = (f32[2,256]{1,0:T(2,128)S(1)}, f32[2,256]{1,0:T(2,128)}, u32[]{:S(2)}) copy-start(f32[2,256]{1,0:T(2,128)} %param.22) | copy-start | bytes 6148
  367.7 29.8 %all-to-all-start.3 = ((f32[32,1,6912]{2,1,0:T(1,128)}), f32[32,1,6912]{2,1,0:T(1,128)S(1)}, u32[]{:S(2)}, u32[]{:S(2)}) async-start(f32[32,1,6912]{2,1,0:T(1,128)} %reshape.735), calls=%async_computation.3 | async-start | bytes 1769472 | tf_op jit(solution)/shard_map/all_to_all | solution.py:62
  421.9 2.6 copy-start.6
  421.9 2.6 copy-start.9
  424.8 5.8 %copy-start.10 = (f32[48,384]{1,0:T(8,128)}, f32[48,384]{1,0:T(8,128)S(1)}, u32[]{:S(2)}) copy-start(f32[48,384]{1,0:T(8,128)S(1)} %get-tuple-element.11) | copy-start | bytes 221188
  467.2 13.2 %all-to-all-start.5 = ((f32[32,1,208]{2,1,0:T(1,128)}), f32[32,1,208]{2,1,0:T(1,128)S(1)}, u32[]{:S(2)}, u32[]{:S(2)}) async-start(f32[32,1,208]{2,1,0:T(1,128)} %reshape.739), calls=%async_computation.5 | async-start | bytes 65536 | tf_op jit(solution)/shard_map/all_to_all | solution.py:106
Sparse Core Ops, SparseCore 0:
  9.8 51.0 all-gather.3
  62.7 56.8 all-gather.5
  225.8 46.5 all-gather.7
where the time goes:
time: 498 us; the launch traced here: 489 us
  waiting for transfers between devices  166 us (33%)
  local copies, waits for them, and re-layouts  140 us (28%)
  blocking collectives  55.1 us (11%)
  matrix products  54.3 us (11%)
  starting transfers between devices  30.7 us (6%)
  other arithmetic  28 us (6%)
  between operations  15.3 us (3%)
    all_gather x2, waiting for transfers between devices, body(): lax.all_gather(grid_field, 'gx', axis=2, tiled=True)  98 us
    unnamed x49, local copies, waits for them, and re-layouts  50.9 us
    all_to_all x1, blocking collectives, body(): lax.all_to_all(turned, 'gy', split_axis=1, concat_axis=2, tiled=True)  42.5 us
    all_to_all x2, waiting for transfers between devices, body(): lax.all_to_all(solved, 'gy', split_axis=2, concat_axis=1, tiled=True)  38.1 us
    dot_general x2, matrix products, body(): jnp.einsum('fyb,ab->fya', lax.all_gather(grid_field, 'gx', axis=2, tiled=...  30.3 us
    dot_general x2, matrix products, body(): solved = jnp.einsum('fxb,ab->fxa', merid_lines, whole_y, precision=highest)  24 us
    all_to_all x4, local copies, waits for them, and re-layouts, body(): lax.all_to_all(solved, 'gy', split_axis=2, concat_axis=1, tiled=True)  22.5 us
    all_to_all x1, waiting for transfers between devices, body(): lax.all_to_all(turned, 'gy', split_axis=1, concat_axis=2, tiled=True)  20.3 us
  transfers between devices with their start and end apart: 7, of which 6 were waited for; matrix products, arithmetic and copies ran while one was open for 8% of the time, Pallas kernels for 0%

commit v1 on v0

--- a/solution.py
+++ b/solution.py
@@ -59,7 +59,10 @@
         turned = jnp.swapaxes(grid_field, 1, 2)
         merid_lines = lax.all_to_all(turned, "gy", split_axis=1, concat_axis=2, tiled=True)
         solved = jnp.einsum("fxb,ab->fxa", merid_lines, whole_y, precision=highest)
-        returned = lax.all_to_all(solved, "gy", split_axis=2, concat_axis=1, tiled=True)
+        returned = jnp.concatenate(
+            lax.all_to_all(jnp.stack(jnp.split(solved, lax.axis_size("gy"), axis=2)), "gy", 0, 0),
+            axis=1,
+        )
         grid_field = sea_open * jnp.swapaxes(returned, 1, 2)
         grid_field = vertical(
             grid_field.reshape(vec_count, kinds, levels, lat_rows, lon_cols), kappa

time: 498 us -> 442 us (0.89)
  local copies, waits for them, and re-layouts: 140 us -> 94.9 us
  blocking collectives: 55.1 us -> 44.3 us
    all_to_all x4 -> x0, local copies, waits for them, and re-layouts: 22.5 us -> none  [body(): lax.all_to_all(solved, 'gy', split_axis=2, concat_axis=1, tiled=True)]
    unnamed x49 -> x119, local copies, waits for them, and re-layouts: 50.9 us -> 32.7 us
    dot_general x2 -> x0, local copies, waits for them, and re-layouts: 17.5 us -> none  [body(): solved = jnp.einsum('fxb,ab->fxa', merid_lines, whole_y, precision=highest)]
    reshape x0 -> x4, local copies, waits for them, and re-layouts: none -> 11.9 us  [body(): jnp.concatenate(lax.all_to_all(jnp.stack(jnp.split(solved, lax.axis_size(...]
    all_to_all x1, blocking collectives: 42.5 us -> 31.8 us  [body(): lax.all_to_all(turned, 'gy', split_axis=1, concat_axis=2, tiled=True)]
  transfers between devices with their start and end apart: 7 -> 7, of which waited for: 6 -> 6; matrix products, arithmetic and copies ran while one was open for 8% -> 9% of each run, Pallas kernels for 0% -> 0%
where the time goes in v1:
time: 442 us; the launch traced here: 433 us
  waiting for transfers between devices  162 us (37%)
  local copies, waits for them, and re-layouts  94.9 us (21%)
  matrix products  54.4 us (12%)
  blocking collectives  44.3 us (10%)
  starting transfers between devices  31.1 us (7%)
  other arithmetic  30.5 us (7%)
  between operations  15.6 us (4%)
    all_gather x2, waiting for transfers between devices, body(): lax.all_gather(grid_field, 'gx', axis=2, tiled=True)  97.4 us
    all_to_all x2, waiting for transfers between devices, body(): lax.all_to_all(jnp.stack(jnp.split(solved, lax.axis_size('gy'), axis=2)),...  35.3 us
    unnamed x119, local copies, waits for them, and re-layouts  32.7 us
    all_to_all x1, blocking collectives, body(): lax.all_to_all(turned, 'gy', split_axis=1, concat_axis=2, tiled=True)  31.8 us
    dot_general x2, matrix products, body(): jnp.einsum('fyb,ab->fya', lax.all_gather(grid_field, 'gx', axis=2, tiled=...  30.3 us
    dot_general x2, matrix products, body(): solved = jnp.einsum('fxb,ab->fxa', merid_lines, whole_y, precision=highest)  24.1 us
    all_to_all x1, waiting for transfers between devices, body(): lax.all_to_all(turned, 'gy', split_axis=1, concat_axis=2, tiled=True)  20.3 us
    all_to_all x2, starting transfers between devices, body(): lax.all_to_all(jnp.stack(jnp.split(solved, lax.axis_size('gy'), axis=2)),...  16.6 us
  transfers between devices with their start and end apart: 7, of which 6 were waited for; matrix products, arithmetic and copies ran while one was open for 9% of the time, Pallas kernels for 0%

profile of v1, /device:TPU:1, one launch (start us, length us, event | category | flops | bytes accessed | tf_op | source)
XLA Modules:
  0.0 433.2 jit_solution(551888291459447017)
XLA Ops:
  10.2 50.7 %all-gather.4.cloned.1.call-done = f32[12,48,3072]{2,1,0:T(8,128)} async-done(((f32[12,48,384]{2,1,0:T(8,128)}), f32[12,48,3072]{2,1,0:T(8,128)}) %all-gather.4.cloned.1.call-update) | async-done | bytes 7077904 | tf_op jit(solution)/shard_map/all_gather | solution.py:55
  60.9 15.1 %fusion.11 = f32[12,384,48]{1,2,0:T(8,128)} fusion(f32[12,48,3072]{2,1,0:T(8,128)} %all-gather.4.cloned.1.call-done, f32[384,3072]{1,0:T(8,128)} %param.17, f32[384,48]{0,1:T(8,128)S(1)} %get-tuple-element.41), kind=kOutput, calls=%fused_computation.16 | convolution fusion | flops 8153948160 | bytes 12754944 | tf_op jit(solution)/shard_map/fyb,ab->fya/dot_general | solution.py:53
  81.7 31.8 %all_to_all.56 = f32[32,1,6912]{2,1,0:T(1,128)S(1)} all-to-all(f32[32,1,6912]{2,1,0:T(1,128)} %reshape.745), channel_id=1, replica_groups=mesh['gx'=8,'gy'=32] {'gy'}, dimensions={0} | all-to-all | bytes 1769472 | tf_op jit(solution)/shard_map/all_to_all | solution.py:60
  113.9 3.7 reduce.1
  126.5 12.2 %fusion.2 = f32[12,12,1536]{2,1,0:T(8,128)S(1)} fusion(f32[12,12,1536]{2,1,0:T(8,128)S(1)} %all_to_all.41, f32[1536,1536]{1,0:T(8,128)} %all-gather.6.cloned.1.call-done), kind=kOutput, calls=%fused_computation.7 | convolution fusion | flops 4076863488 | bytes 11206656 | tf_op jit(solution)/shard_map/fxb,ab->fxa/dot_general | solution.py:61
  144.7 8.1 %all-to-all-start.1 = ((f32[32,1,6912]{2,1,0:T(1,128)}), f32[32,1,6912]{2,1,0:T(1,128)S(1)}, u32[]{:S(2)}, u32[]{:S(2)}) async-start(f32[32,1,6912]{2,1,0:T(1,128)} %reshape.747), calls=%async_computation.1 | async-start | bytes 1769472 | tf_op jit(solution)/shard_map/all_to_all | solution.py:63
  159.0 15.3 %all-to-all-done.1 = f32[32,1,6912]{2,1,0:T(1,128)S(1)} async-done(((f32[32,1,6912]{2,1,0:T(1,128)}), f32[32,1,6912]{2,1,0:T(1,128)S(1)}, u32[]{:S(2)}, u32[]{:S(2)}) %all-to-all-start.1) | async-done | bytes 884768 | tf_op jit(solution)/shard_map/all_to_all | solution.py:63
  174.2 3.7 reduce.2
  183.0 4.0 reshape.664
  192.4 46.7 %all-gather.8.cloned.1.call-done = f32[12,48,3072]{2,1,0:T(8,128)} async-done(((f32[12,48,384]{2,1,0:T(8,128)}), f32[12,48,3072]{2,1,0:T(8,128)}) %all-gather.8.cloned.1.call-update) | async-done | bytes 7077904 | tf_op jit(solution)/shard_map/all_gather | solution.py:55
  239.1 15.1 %fusion.17 = f32[12,384,48]{1,2,0:T(8,128)} fusion(f32[12,48,3072]{2,1,0:T(8,128)} %all-gather.8.cloned.1.call-done, f32[384,3072]{1,0:T(8,128)} %param.17, f32[384,48]{0,1:T(8,128)S(1)} %copy-done.12), kind=kOutput, calls=%fused_computation.18 | convolution fusion | flops 8153948160 | bytes 12754944 | tf_op jit(solution)/shard_map/fyb,ab->fya/dot_general | solution.py:53
  259.8 10.0 %all-to-all-start.2 = ((f32[32,1,6912]{2,1,0:T(1,128)}), f32[32,1,6912]{2,1,0:T(1,128)S(1)}, u32[]{:S(2)}, u32[]{:S(2)}) async-start(f32[32,1,6912]{2,1,0:T(1,128)} %reshape.749), calls=%async_computation.2 | async-start | bytes 1769472 | tf_op jit(solution)/shard_map/all_to_all | solution.py:60
  270.9 20.3 %all-to-all-done.2 = f32[32,1,6912]{2,1,0:T(1,128)S(1)} async-done(((f32[32,1,6912]{2,1,0:T(1,128)}), f32[32,1,6912]{2,1,0:T(1,128)S(1)}, u32[]{:S(2)}, u32[]{:S(2)}) %all-to-all-start.2) | async-done | bytes 884768 | tf_op jit(solution)/shard_map/all_to_all | solution.py:60
  291.2 3.7 reduce.3
  303.7 12.0 %fusion = f32[12,12,1536]{2,1,0:T(8,128)S(1)} fusion(f32[12,12,1536]{2,1,0:T(8,128)S(1)} %all_to_all.46, f32[1536,1536]{1,0:T(8,128)} %all-gather.6.cloned.1.call-done), kind=kOutput, calls=%fused_computation.5 | convolution fusion | flops 4076863488 | bytes 11206656 | tf_op jit(solution)/shard_map/fxb,ab->fxa/dot_general | solution.py:61
  321.8 8.5 %all-to-all-start.3 = ((f32[32,1,6912]{2,1,0:T(1,128)}), f32[32,1,6912]{2,1,0:T(1,128)S(1)}, u32[]{:S(2)}, u32[]{:S(2)}) async-start(f32[32,1,6912]{2,1,0:T(1,128)} %reshape.751), calls=%async_computation.3 | async-start | bytes 1769472 | tf_op jit(solution)/shard_map/all_to_all | solution.py:63
  331.7 20.1 %all-to-all-done.3 = f32[32,1,6912]{2,1,0:T(1,128)S(1)} async-done(((f32[32,1,6912]{2,1,0:T(1,128)}), f32[32,1,6912]{2,1,0:T(1,128)S(1)}, u32[]{:S(2)}, u32[]{:S(2)}) %all-to-all-start.3) | async-done | bytes 884768 | tf_op jit(solution)/shard_map/all_to_all | solution.py:63
  351.7 3.8 reduce.4
  360.3 4.0 reshape.668
  369.2 5.7 %copy.100 = f32[1,13,48,384]{1,3,2,0:T(8,128)} copy(f32[1,13,48,384]{3,2,1,0:T(8,128)S(1)} %pad_maximum_fusion) | data formatting | bytes 1916928 | tf_op jit(solution)/shard_map/concatenate | solution.py:78
  384.7 12.1 %scatter_fusion = f32[2,13,256]{1,2,0:T(8,128)S(1)} fusion(f32[2,13,256]{1,2,0:T(8,128)S(1)} %broadcast_in_dim.15, s32[256]{0:T(256)S(1)} %bitcast.422, f32[256,13]{1,0:T(8,128)S(1)} %copy.105), kind=kCustom, calls=%fused_computation.4 | custom fusion | bytes 41984 | tf_op jit(solution)/shard_map/scatter | solution.py:106
  397.2 12.6 %all_to_all.57 = f32[8,1,832]{2,1,0:T(1,128)S(1)} all-to-all(f32[8,1,832]{2,1,0:T(1,128)S(1)} %reshape.753), channel_id=1, replica_groups=mesh['gx'=8,'gy'=32] {'gx'}, dimensions={0} | all-to-all | bytes 53248 | tf_op jit(solution)/shard_map/all_to_all | solution.py:110
  411.5 4.4 %all-to-all-start.5 = ((f32[32,1,208]{2,1,0:T(1,128)}), f32[32,1,208]{2,1,0:T(1,128)S(1)}, u32[]{:S(2)}, u32[]{:S(2)}) async-start(f32[32,1,208]{2,1,0:T(1,128)} %reshape.755), calls=%async_computation.5 | async-start | bytes 65536 | tf_op jit(solution)/shard_map/all_to_all | solution.py:109
  416.9 7.8 %all-to-all-done.5 = f32[32,1,208]{2,1,0:T(1,128)S(1)} async-done(((f32[32,1,208]{2,1,0:T(1,128)}), f32[32,1,208]{2,1,0:T(1,128)S(1)}, u32[]{:S(2)}, u32[]{:S(2)}) %all-to-all-start.5) | async-done | bytes 26656 | tf_op jit(solution)/shard_map/all_to_all | solution.py:109
  (191 shorter events, 86.2 us)
Async XLA Ops:
  7.2 53.7 %all-gather.4.cloned.1.call-start = ((), (), s32[]{:S(2)}) async-start(), calls=%async_computation.6 | async-start | bytes 7962624 | tf_op jit(solution)/shard_map/all_gather | solution.py:55
  7.9 118.6 %all-gather.6.cloned.1.call-start = ((), (), s32[]{:S(2)}) async-start(), calls=%async_computation.7 | async-start | bytes 10616832 | tf_op jit(solution)/shard_map/all_gather | solution.py:51
  10.2 50.7 %copy-start.11 = (f32[384,48]{0,1:T(8,128)}, f32[384,48]{0,1:T(8,128)S(1)}, u32[]{:S(2)}) copy-start(f32[384,48]{0,1:T(8,128)S(1)} %get-tuple-element.41) | copy-start | bytes 221188
  141.3 13.2 %copy-start = (f32[5,48,384]{2,1,0:T(8,128)S(1)}, f32[5,48,384]{2,1,0:T(8,128)}, u32[]{:S(2)}) copy-start(f32[5,48,384]{2,1,0:T(8,128)} %param.14) | copy-start | bytes 1105924
  144.7 12.8 %copy-start.1 = (f32[5,48,384]{2,1,0:T(8,128)S(1)}, f32[5,48,384]{2,1,0:T(8,128)}, u32[]{:S(2)}) copy-start(f32[5,48,384]{2,1,0:T(8,128)} %param.14) | copy-start | bytes 1105924
  144.7 29.5 %all-to-all-start.1 = ((f32[32,1,6912]{2,1,0:T(1,128)}), f32[32,1,6912]{2,1,0:T(1,128)S(1)}, u32[]{:S(2)}, u32[]{:S(2)}) async-start(f32[32,1,6912]{2,1,0:T(1,128)} %reshape.747), calls=%async_computation.1 | async-start | bytes 1769472 | tf_op jit(solution)/shard_map/all_to_all | solution.py:63
  152.8 86.2 %all-gather.8.cloned.1.call-start = ((), (), s32[]{:S(2)}) async-start(), calls=%async_computation.8 | async-start | bytes 7962624 | tf_op jit(solution)/shard_map/all_gather | solution.py:55
  155.3 19.0 %copy-start.8 = (f32[48,384]{1,0:T(8,128)}, f32[48,384]{1,0:T(8,128)S(1)}, u32[]{:S(2)}) copy-start(f32[48,384]{1,0:T(8,128)S(1)} %get-tuple-element.25) | copy-start | bytes 221188
  183.0 4.0 copy-start.4
  189.7 49.3 %copy-start.12 = (f32[384,48]{0,1:T(8,128)S(1)}, f32[384,48]{0,1:T(8,128)}, u32[]{:S(2)}) copy-start(f32[384,48]{0,1:T(8,128)} %copy-done.11) | copy-start | bytes 221188
  256.5 14.0 %copy-start.15 = (s32[256,1]{0,1:T(1,128)S(1)}, s32[256,1]{0,1:T(1,128)}, u32[]{:S(2)}) copy-start(s32[256,1]{0,1:T(1,128)} %param.20) | copy-start | bytes 3076
  259.8 31.4 %all-to-all-start.2 = ((f32[32,1,6912]{2,1,0:T(1,128)}), f32[32,1,6912]{2,1,0:T(1,128)S(1)}, u32[]{:S(2)}, u32[]{:S(2)}) async-start(f32[32,1,6912]{2,1,0:T(1,128)} %reshape.749), calls=%async_computation.2 | async-start | bytes 1769472 | tf_op jit(solution)/shard_map/all_to_all | solution.py:60
  270.8 20.4 %copy-start.9 = (s32[256,2,128]{0,1,2:T(2,128)}, s32[256,2,128]{0,1,2:T(2,128)S(1)}, u32[]{:S(2)}) copy-start(s32[256,2,128]{0,1,2:T(2,128)S(1)} %fusion.23) | copy-start | bytes 786436
  270.9 29.7 %copy-start.16 = (s32[256,3]{0,1:T(4,128)}, s32[256,3]{0,1:T(4,128)S(1)}, u32[]{:S(2)}) copy-start(s32[256,3]{0,1:T(4,128)S(1)} %reduce-window.9) | copy-start | bytes 9220
  318.2 12.1 %slice-start = ((s32[256,3]{0,1:T(4,128)}), s32[256,2]{0,1:T(2,128)S(1)}, s32[]{:S(2)}) async-start(s32[256,3]{0,1:T(4,128)} %copy-done.16), calls=%async_computation.9 | async-start | bytes 4096 | tf_op jit(solution)/shard_map/slice.1
  318.4 13.1 %copy-start.19 = (f32[2,6]{1,0:T(2,128)S(1)}, f32[2,6]{1,0:T(2,128)}, u32[]{:S(2)}) copy-start(f32[2,6]{1,0:T(2,128)} %param.19) | copy-start | bytes 148
  318.5 13.1 %copy-start.17 = (s32[256]{0:T(256)S(1)}, s32[256]{0:T(256)}, u32[]{:S(2)}) copy-start(s32[256]{0:T(256)} %param.21) | copy-start | bytes 3076
  318.5 13.2 %copy-start.18 = (f32[2,256]{1,0:T(2,128)S(1)}, f32[2,256]{1,0:T(2,128)}, u32[]{:S(2)}) copy-start(f32[2,256]{1,0:T(2,128)} %param.22) | copy-start | bytes 6148
  321.8 30.0 %all-to-all-start.3 = ((f32[32,1,6912]{2,1,0:T(1,128)}), f32[32,1,6912]{2,1,0:T(1,128)S(1)}, u32[]{:S(2)}, u32[]{:S(2)}) async-start(f32[32,1,6912]{2,1,0:T(1,128)} %reshape.751), calls=%async_computation.3 | async-start | bytes 1769472 | tf_op jit(solution)/shard_map/all_to_all | solution.py:63
  360.3 4.0 copy-start.5
  367.1 1.8 copy-start.10
  367.1 1.8 copy-start.13
  369.1 5.8 %copy-start.14 = (f32[48,384]{1,0:T(8,128)}, f32[48,384]{1,0:T(8,128)S(1)}, u32[]{:S(2)}) copy-start(f32[48,384]{1,0:T(8,128)S(1)} %get-tuple-element.11) | copy-start | bytes 221188
  411.5 13.2 %all-to-all-start.5 = ((f32[32,1,208]{2,1,0:T(1,128)}), f32[32,1,208]{2,1,0:T(1,128)S(1)}, u32[]{:S(2)}, u32[]{:S(2)}) async-start(f32[32,1,208]{2,1,0:T(1,128)} %reshape.755), calls=%async_computation.5 | async-start | bytes 65536 | tf_op jit(solution)/shard_map/all_to_all | solution.py:109
  (4 other events, 4.7 us)
Sparse Core Ops, SparseCore 0:
  9.8 51.0 all-gather.3
  62.7 56.8 all-gather.5
  192.5 46.5 all-gather.7
